TPU v7x, 512 devices: a whole 4x8x8 slice. The times are simulated.
512 devices in a mesh: row: 16 (over z, core), col: 32 (over x, y).
Axes of the slice: x: 4, y: 8, z: 8, core: 2. Of those that a mesh axis runs over, the one named last changes fastest.
Arguments:
- state_fields: bfloat16 [4, 16, 16, 16, 32, 256], P(None, None, None, 'row', 'col'), may hold values from -6 to 6
- leaf_solve: float32 [256, 256], replicated, may hold values from -0.375 to 0.375
- leaf_flux: float32 [64, 256], replicated, may hold values from -0.375 to 0.375
- lift_edges: float32 [64, 128], replicated, may hold values from -4 to 4
- lift_leaves: float32 [256, 128], replicated, may hold values from -0.046875 to 0.046875
- merge_interface: float32 [5, 128, 128], replicated, may hold values from -0.25 to 0.25
- merge_parent: float32 [5, 256, 128], replicated, may hold values from -0.375 to 0.375
- split_child: float32 [5, 128, 256], replicated, may hold values from -0.5 to 0.5
- top_inverse: float32 [2048, 2048], P(None, 'row'), may hold values from -0.125 to 0.125
- spread_edges: float32 [64, 128], replicated, may hold values from -4 to 4
- spread_leaves: float32 [256, 128], replicated, may hold values from -0.5 to 0.5
- leaf_extend: float32 [256, 64], replicated, may hold values from -0.375 to 0.375
Outputs:
- new_fields: bfloat16 [4, 16, 16, 16, 32, 256], P(None, None, None, 'row', 'col')
All inputs are finite; a program needn't handle non-finite values.
Results may differ from a plain program's by a relative error of at most 0.0035.
Values may be sent and summed in bfloat16 or wider, within the bound.
A program may use at most 64 MiB of HBM per device.

v0:
```python
import jax
import jax.numpy as jnp
import numpy as np
from jax import lax
from jax.sharding import PartitionSpec as P

SKEL = 128
LR = 4
LC = 64
advect_scale = 0.01
full_precision = lax.Precision.HIGHEST


def extended(x, sides, width):
    for axis, dim in sides:
        devices, length = (lax.axis_size(axis), x.shape[dim])
        up = [(i, (i + 1) % devices) for i in range(devices)]
        down = [(j, i) for i, j in up]
        last = lax.slice_in_dim(x, length - width, length, axis=dim)
        first = lax.slice_in_dim(x, 0, width, axis=dim)
        before = lax.ppermute(last, axis, up)
        after = lax.ppermute(first, axis, down)
        x = jnp.concatenate([before, x, after], axis=dim)
    return x


def partner_2(block, axis, stride):
    count = lax.axis_size(axis)
    route = []
    for low in range(count):
        high = low | 1 << stride
        if high != low and high < count:
            route += [(low, high), (high, low)]
    return lax.ppermute(block, axis, route)


def chebyshev_matrix(node_count):
    points = np.arange(node_count)
    grid_x = np.cos(np.pi * points / (node_count - 1))
    weights = np.where(points == 0, 2.0, np.where(points == node_count - 1, 2.0, 1.0))
    parity = np.where((points[:, None] + points[None, :]) % 2 == 0, 1.0, -1.0)
    identity = np.eye(node_count)
    spacing = grid_x[:, None] - grid_x[None, :] + identity
    off_diagonal = weights[:, None] / weights[None, :] * parity / spacing * (1.0 - identity)
    result_matrix = off_diagonal - identity * off_diagonal.sum(axis=1)[:, None]
    return jnp.asarray(result_matrix, dtype=jnp.float32)


def tendency(values):
    derivative = chebyshev_matrix(values.shape[1])
    along_rows = jnp.einsum("ik,fkjrc->fijrc", derivative, values, precision=full_precision)
    along_cols = jnp.einsum("jk,fikrc->fijrc", derivative, values, precision=full_precision)
    return advect_scale * (values[0:1] * along_rows + values[1:2] * along_cols)


def average_rows(values, north_in, south_in):
    above = jnp.concatenate([north_in, values[:, -1, :, :-1, :]], axis=2)
    below = jnp.concatenate([values[:, 0, :, 1:, :], south_in], axis=2)
    first_row = (values[:, 0] + above) * 0.5
    last_row = (values[:, -1] + below) * 0.5
    return jnp.concatenate([first_row[:, None], values[:, 1:-1], last_row[:, None]], axis=1)


def average_cols(values, west_in, east_in):
    left_side = jnp.concatenate([west_in, values[:, :, -1, :, :-1]], axis=3)
    right_side = jnp.concatenate([values[:, :, 0, :, 1:], east_in], axis=3)
    first_col = (values[:, :, 0] + left_side) * 0.5
    last_col = (values[:, :, -1] + right_side) * 0.5
    return jnp.concatenate(
        [first_col[:, :, None], values[:, :, 1:-1], last_col[:, :, None]], axis=2
    )


def local(
    state_fields,
    leaf_solve,
    leaf_flux,
    lift_edges,
    lift_leaves,
    merge_interface,
    merge_parent,
    split_child,
    top_inverse,
    spread_edges,
    spread_leaves,
    leaf_extend,
):
    field_count = state_fields.shape[0]
    node_count = state_fields.shape[1]
    leaf_total = state_fields.shape[-1]
    local_grid = state_fields.reshape(field_count, node_count, node_count, LR, LC)
    widened = extended(local_grid, (("row", 3), ("col", 4)), 1)
    pushed = tendency(widened.astype(jnp.float32))
    rows_done = average_rows(pushed, pushed[:, -1][:, :, :1, :], pushed[:, 0][:, :, -1:, :])
    both_done = average_cols(
        rows_done, rows_done[:, :, -1][:, :, :, :1], rows_done[:, :, 0][:, :, :, -1:]
    )
    averaged = both_done[:, :, :, 1:-1, 1:-1]
    values = local_grid.astype(jnp.float32)
    source = (values - averaged).reshape(field_count, node_count * node_count, leaf_total)
    particular = jnp.einsum("nm,fml->fnl", leaf_solve, source, precision=full_precision)
    edge_flux = jnp.einsum("em,fml->fel", leaf_flux, source, precision=full_precision)
    lifted = jnp.einsum("fel,lb->feb", edge_flux, lift_leaves, precision=full_precision)
    skeleton = jnp.sum(lifted * lift_edges[None], axis=1)
    column = lax.axis_index("col")
    level_count = lax.axis_size("col").bit_length() - 1
    interfaces = []
    for merge_level in range(level_count):
        stride = 1 << merge_level
        partner = partner_2(skeleton, "col", merge_level)
        on_left = column // stride % 2 == 0
        left_half = jnp.where(on_left, skeleton, partner)
        right_half = jnp.where(on_left, partner, skeleton)
        interfaces.append(
            jnp.dot(right_half - left_half, merge_interface[merge_level], precision=full_precision)
        )
        joined = jnp.concatenate([left_half, right_half], axis=-1)
        skeleton = jnp.dot(joined, merge_parent[merge_level], precision=full_precision)
    shard_piece = lax.all_gather(skeleton[None], "row", axis=0, tiled=True)
    piece_rows = shard_piece.shape[0]
    top_rows = top_inverse
    top_rows = top_rows.reshape(piece_rows, SKEL, SKEL)
    boundary = jnp.einsum("gfb,gbc->fc", shard_piece, top_rows, precision=full_precision)
    for merge_level in reversed(range(level_count)):
        stride = 1 << merge_level
        child_map = split_child[merge_level]
        left_half = (
            jnp.dot(boundary, child_map[:, :SKEL], precision=full_precision)
            + interfaces[merge_level]
        )
        right_half = (
            jnp.dot(boundary, child_map[:, SKEL:], precision=full_precision)
            + interfaces[merge_level]
        )
        boundary = jnp.where(column // stride % 2 == 0, left_half, right_half)
    weighted = boundary[:, None, :] * spread_edges[None]
    spread = jnp.einsum("feb,lb->fel", weighted, spread_leaves, precision=full_precision)
    solved = particular + jnp.einsum("ne,fel->fnl", leaf_extend, spread, precision=full_precision)
    return solved.reshape(field_count, node_count, node_count, 1, 1, leaf_total).astype(
        jnp.bfloat16
    )


def solution(mesh):
    in_specs = (
        P(None, None, None, "row", "col", None),
        P(),
        P(),
        P(),
        P(),
        P(),
        P(),
        P(),
        P(None, "row"),
        P(),
        P(),
        P(),
    )
    out_specs = P(None, None, None, "row", "col", None)
    return jax.shard_map(local, mesh=mesh, in_specs=in_specs, out_specs=out_specs, check_vma=False)
```

profile of v0, /device:TPU:1, one launch (start us, length us, event | category | flops | bytes accessed | tf_op | source)
XLA Modules:
  0.0 127.9 jit_solution(2190358243321352747)
XLA Ops:
  0.0 2.1 %reshape.38 = bf16[4,16,16,4,64]{4,3,2,1,0:T(4,128)(2,1)S(1)} reshape(bf16[4,16,16,1,1,256]{5,2,4,3,1,0:T(8,128)(2,1)} %param.13) | data formatting | bytes 1048576 | tf_op jit(solution)/shard_map/reshape | solution.py:91
  2.1 0.7 fusion.100
  2.9 0.2 copy.84
  3.1 3.5 %collective-permute-start = (bf16[4,16,16,1,64]{4,1,3,2,0:T(8,128)(2,1)S(1)}, bf16[4,16,16,1,64]{4,1,3,2,0:T(8,128)(2,1)S(1)}, u32[]{:S(2)}, u32[]{:S(2)}) collective-permute-start(bf16[4,16,16,1,64]{4,1,3,2,0:T(8,128)(2,1)S(1)} %copy.84), channel_id=1, source_target_pairs={{0,32},{32,64},{64,96},{96,128},{128,160},{160,192},{192,224},{224... | collective-permute-start | bytes 393224 | tf_op jit(solution)/shard_map/ppermute | solution.py:21
  6.5 0.2 copy.85
  6.7 3.4 %collective-permute-start.1 = (bf16[4,16,16,1,64]{4,1,3,2,0:T(8,128)(2,1)S(1)}, bf16[4,16,16,1,64]{4,1,3,2,0:T(8,128)(2,1)S(1)}, u32[]{:S(2)}, u32[]{:S(2)}) collective-permute-start(bf16[4,16,16,1,64]{4,1,3,2,0:T(8,128)(2,1)S(1)} %copy.85), channel_id=1, source_target_pairs={{32,0},{64,32},{96,64},{128,96},{160,128},{192,160},{224,192},{256... | collective-permute-start | bytes 393224 | tf_op jit(solution)/shard_map/ppermute | solution.py:22
  10.1 0.8 collective-permute-done
  11.0 1.3 %constant_dynamic-update-slice_fusion.1 = bf16[4,16,16,6,64]{4,1,3,2,0:T(8,128)(2,1)S(1)} fusion(bf16[4,16,16,6,64]{4,1,3,2,0:T(8,128)(2,1)S(1)} %constant_dynamic-update-slice_fusion.2, bf16[4,16,16,4,64]{4,3,2,1,0:T(4,128)(2,1)S(1)} %reshape.38), kind=kLoop, calls=%fused_computation.110 | loop fusion | bytes 2097152
  12.2 0.3 collective-permute-done.1
  12.6 2.4 %fusion.99 = (bf16[4,16,16,6,1]{4,1,3,2,0:T(8,128)(2,1)}, bf16[4,16,16,6,1]{4,1,3,2,0:T(8,128)(2,1)}) fusion(bf16[4,16,16,6,64]{4,1,3,2,0:T(8,128)(2,1)S(1)} %constant_dynamic-update-slice_fusion), kind=kLoop, calls=%fused_computation.150 | loop fusion | bytes 49152 | tf_op jit(solution)/shard_map/slice | solution.py:19
  14.9 3.7 %copy.58 = bf16[4,16,16,6,1]{2,1,4,3,0:T(8,128)(2,1)S(1)} copy(bf16[4,16,16,6,1]{4,1,3,2,0:T(8,128)(2,1)} %get-tuple-element.19) | data formatting | bytes 24576 | tf_op jit(solution)/shard_map/slice | solution.py:19
  18.6 3.2 %collective-permute-start.2 = (bf16[4,16,16,6,1]{2,1,4,3,0:T(8,128)(2,1)S(1)}, bf16[4,16,16,6,1]{2,1,4,3,0:T(8,128)(2,1)}, u32[]{:S(2)}, u32[]{:S(2)}) collective-permute-start(bf16[4,16,16,6,1]{2,1,4,3,0:T(8,128)(2,1)S(1)} %copy.58), channel_id=1, source_target_pairs={{0,1},{1,2},{2,3},{3,4},{4,5},{5,6},{6,7},{7,8},{8,9},{9,10},{10,1... | collective-permute-start | bytes 36872 | tf_op jit(solution)/shard_map/ppermute | solution.py:21
  21.8 4.2 %copy.59 = bf16[4,16,16,6,1]{2,1,4,3,0:T(8,128)(2,1)} copy(bf16[4,16,16,6,1]{4,1,3,2,0:T(8,128)(2,1)} %get-tuple-element.20) | data formatting | bytes 24576 | tf_op jit(solution)/shard_map/slice | solution.py:20
  26.0 6.0 %collective-permute-start.3 = (bf16[4,16,16,6,1]{2,1,4,3,0:T(8,128)(2,1)}, bf16[4,16,16,6,1]{2,1,4,3,0:T(8,128)(2,1)}, u32[]{:S(2)}, u32[]{:S(2)}) collective-permute-start(bf16[4,16,16,6,1]{2,1,4,3,0:T(8,128)(2,1)} %copy.59), channel_id=1, source_target_pairs={{1,0},{2,1},{3,2},{4,3},{5,4},{6,5},{7,6},{8,7},{9,8},{10,9},{11,1... | collective-permute-start | bytes 36872 | tf_op jit(solution)/shard_map/ppermute | solution.py:22
  32.2 4.6 %copy.60 = bf16[4,16,16,6,1]{4,1,3,2,0:T(8,128)(2,1)} copy(bf16[4,16,16,6,1]{2,1,4,3,0:T(8,128)(2,1)} %collective-permute-done.2) | data formatting | bytes 24576 | tf_op jit(solution)/shard_map/ppermute | solution.py:21
  36.8 4.6 %copy.61 = bf16[4,16,16,6,1]{4,1,3,2,0:T(8,128)(2,1)} copy(bf16[4,16,16,6,1]{2,1,4,3,0:T(8,128)(2,1)} %collective-permute-done.3) | data formatting | bytes 24576 | tf_op jit(solution)/shard_map/ppermute | solution.py:22
  41.4 3.8 %fusion.96 = (f32[4,16,16,6,66]{4,1,3,2,0:T(8,128)S(1)}, bf16[4,16,16,6,66]{4,1,3,2,0:T(8,128)(2,1)S(1)}) fusion(bf16[4,16,16,6,1]{4,1,3,2,0:T(8,128)(2,1)} %copy.61, bf16[4,16,16,6,64]{4,1,3,2,0:T(8,128)(2,1)} %copy-done.2, bf16[4,16,16,6,1]{4,1,3,2,0:T(8,128)(2,1)} %copy.60), kind=kLoop, calls=%fused_computation.147 | loop fusion | flops 2838528 | bytes 3244032 | tf_op jit(solution)/shard_map/convert_element_type | solution.py:93
  45.3 0.6 copy-done.14
  45.9 1.5 %fusion.3 = f32[4,16,6,66,16]{3,4,2,1,0:T(8,128)S(1)} fusion(f32[16,16,1,1,1]{1,0,4,3,2:T(8,128)S(1)} %copy-done.14, bf16[4,16,16,6,66]{4,1,3,2,0:T(8,128)(2,1)S(1)} %get-tuple-element.6), kind=kOutput, calls=%fused_computation.9 | convolution fusion | flops 77856768 | bytes 2434048 | tf_op jit(solution)/shard_map/jk,fikrc->fijrc/dot_general | solution.py:52
  47.4 3.5 %fusion.1 = f32[4,16,16,6,66]{4,1,3,2,0:T(8,128)S(1)} fusion(f32[4,16,6,66,16]{3,4,2,1,0:T(8,128)S(1)} %fusion.3, bf16[4,16,16,6,66]{4,1,3,2,0:T(8,128)(2,1)S(1)} %get-tuple-element.6, f32[16,16,1,1,1]{1,0,4,3,2:T(8,128)S(1)} %copy-done.14, f32[16,16,6,66]{3,0,2,1:T(8,128)S(1)} %get-tuple-element.18, f32[16,16,6,66]{3,0,2,1:T(8,128)S(1)} %get-tuple-element.17), kind=kOutput, calls=%fused_computation.3 | convolution fusion | flops 79478784 | bytes 4867072 | tf_op jit(solution)/shard_map/ik,fkjrc->fijrc/dot_general | solution.py:51
  50.9 0.3 fusion.97
  51.2 0.2 fusion.98
  51.4 0.4 slice.198
  51.8 0.7 fusion.22
  52.5 0.8 pad_maximum_fusion
  53.5 1.6 %copy-done.3 = f32[4,16,16,6,66]{4,1,3,2,0:T(8,128)} copy-done((f32[4,16,16,6,66]{4,1,3,2,0:T(8,128)}, f32[4,16,16,6,66]{4,1,3,2,0:T(8,128)S(1)}, u32[]{:S(2)}) %copy-start.3) | copy-done | bytes 1622040
  55.2 0.2 copy.70
  55.4 0.2 copy.71
  55.7 0.2 copy.68
  55.9 0.2 copy.69
  56.1 1.7 %fusion.19 = (f32[4,16,1,6,66]{4,1,3,2,0:T(8,128)S(1)}, f32[4,16,1,6,66]{4,1,3,2,0:T(8,128)S(1)}) fusion(f32[4,1,16,6,66]{4,1,3,2,0:T(1,128)S(1)} %get-tuple-element.12, f32[4,14,16,6,66]{4,1,3,2,0:T(8,128)} %copy-done.1, f32[4,1,16,6,66]{4,1,3,2,0:T(1,128)S(1)} %get-tuple-element.11, f32[4,16,1,6,1]{4,1,3,2,0:T(8,128)S(1)} %copy.69, ...), kind=kLoop, calls=%fused_computation.45 | loop fusion | flops 354816 | bytes 1827840 | tf_op jit(solution)/shard_map/mul | solution.py:67
  57.8 0.4 slice-done
  58.2 1.5 %fusion.2 = f32[4,16,16,4,64]{4,1,3,2,0:T(8,128)S(1)} fusion(f32[4,16,1,6,66]{4,1,3,2,0:T(8,128)S(1)} %get-tuple-element.8, f32[4,16,14,6,66]{4,1,3,2,0:T(8,128)S(1)} %slice-done, f32[4,16,1,6,66]{4,1,3,2,0:T(8,128)S(1)} %get-tuple-element.7, bf16[4,16,16,4,64]{4,3,2,1,0:T(4,128)(2,1)S(1)} %reshape.38), kind=kLoop, calls=%fused_computation.6 | loop fusion | flops 1048576 | bytes 3194880 | tf_op jit(solution)/shard_map/sub | solution.py:100
  59.7 2.4 %copy.72 = f32[4,16,16,4,64]{4,3,2,1,0:T(4,128)} copy(f32[4,16,16,4,64]{4,1,3,2,0:T(8,128)S(1)} %fusion.2) | data formatting | bytes 2097152 | tf_op jit(solution)/shard_map/sub | solution.py:100
  62.1 2.5 %reshape.39 = f32[4,256,256]{2,1,0:T(8,128)S(1)} reshape(f32[4,16,16,4,64]{4,3,2,1,0:T(4,128)} %copy.72) | data formatting | bytes 2097152 | tf_op jit(solution)/shard_map/reshape | solution.py:100
  64.7 0.8 convolution_bitcast_fusion
  65.5 0.4 fusion.6
  65.9 2.1 %collective-permute-start.4 = (f32[4,128]{1,0:T(4,128)S(1)}, f32[4,128]{1,0:T(4,128)S(1)}, u32[]{:S(2)}, u32[]{:S(2)}) collective-permute-start(f32[4,128]{1,0:T(4,128)S(1)} %fusion.6), channel_id=1, source_target_pairs={{0,1},{1,0},{2,3},{3,2},{4,5},{5,4},{6,7},{7,6},{8,9},{9,8},{10,11... | collective-permute-start | bytes 6152 | tf_op jit(solution)/shard_map/ppermute | solution.py:34
  68.0 1.1 fusion.12
  69.1 1.3 %collective-permute-done.4 = f32[4,128]{1,0:T(4,128)S(1)} collective-permute-done((f32[4,128]{1,0:T(4,128)S(1)}, f32[4,128]{1,0:T(4,128)S(1)}, u32[]{:S(2)}, u32[]{:S(2)}) %collective-permute-start.4) | collective-permute-done | bytes 2080 | tf_op jit(solution)/shard_map/ppermute | solution.py:34
  70.4 0.2 fusion.33
  70.6 1.9 %collective-permute-start.5 = (f32[4,128]{1,0:T(4,128)S(1)}, f32[4,128]{1,0:T(4,128)S(1)}, u32[]{:S(2)}, u32[]{:S(2)}) collective-permute-start(f32[4,128]{1,0:T(4,128)S(1)} %fusion.33), channel_id=1, source_target_pairs={{0,2},{2,0},{1,3},{3,1},{4,6},{6,4},{5,7},{7,5},{8,10},{10,8},{9,1... | collective-permute-start | bytes 6152 | tf_op jit(solution)/shard_map/ppermute | solution.py:34
  72.7 3.1 %collective-permute-done.5 = f32[4,128]{1,0:T(4,128)S(1)} collective-permute-done((f32[4,128]{1,0:T(4,128)S(1)}, f32[4,128]{1,0:T(4,128)S(1)}, u32[]{:S(2)}, u32[]{:S(2)}) %collective-permute-start.5) | collective-permute-done | bytes 2080 | tf_op jit(solution)/shard_map/ppermute | solution.py:34
  75.8 0.2 fusion.31
  76.0 4.7 %collective-permute-start.6 = (f32[4,128]{1,0:T(4,128)S(1)}, f32[4,128]{1,0:T(4,128)S(1)}, u32[]{:S(2)}, u32[]{:S(2)}) collective-permute-start(f32[4,128]{1,0:T(4,128)S(1)} %fusion.31), channel_id=1, source_target_pairs={{0,4},{4,0},{1,5},{5,1},{2,6},{6,2},{3,7},{7,3},{8,12},{12,8},{9,1... | collective-permute-start | bytes 6152 | tf_op jit(solution)/shard_map/ppermute | solution.py:34
  80.9 3.3 %collective-permute-done.6 = f32[4,128]{1,0:T(4,128)S(1)} collective-permute-done((f32[4,128]{1,0:T(4,128)S(1)}, f32[4,128]{1,0:T(4,128)S(1)}, u32[]{:S(2)}, u32[]{:S(2)}) %collective-permute-start.6) | collective-permute-done | bytes 2080 | tf_op jit(solution)/shard_map/ppermute | solution.py:34
  84.4 1.9 %collective-permute-start.7 = (f32[4,128]{1,0:T(4,128)S(1)}, f32[4,128]{1,0:T(4,128)S(1)}, u32[]{:S(2)}, u32[]{:S(2)}) collective-permute-start(f32[4,128]{1,0:T(4,128)S(1)} %fusion.29), channel_id=1, source_target_pairs={{0,8},{8,0},{1,9},{9,1},{2,10},{10,2},{3,11},{11,3},{4,12},{12,4},... | collective-permute-start | bytes 6152 | tf_op jit(solution)/shard_map/ppermute | solution.py:34
  86.5 2.2 %collective-permute-done.7 = f32[4,128]{1,0:T(4,128)S(1)} collective-permute-done((f32[4,128]{1,0:T(4,128)S(1)}, f32[4,128]{1,0:T(4,128)S(1)}, u32[]{:S(2)}, u32[]{:S(2)}) %collective-permute-start.7) | collective-permute-done | bytes 2080 | tf_op jit(solution)/shard_map/ppermute | solution.py:34
  88.7 0.2 fusion.27
  88.9 2.8 %collective-permute-start.8 = (f32[4,128]{1,0:T(4,128)S(1)}, f32[4,128]{1,0:T(4,128)S(1)}, u32[]{:S(2)}, u32[]{:S(2)}) collective-permute-start(f32[4,128]{1,0:T(4,128)S(1)} %fusion.27), channel_id=1, source_target_pairs={{0,16},{16,0},{1,17},{17,1},{2,18},{18,2},{3,19},{19,3},{4,20},{20... | collective-permute-start | bytes 6152 | tf_op jit(solution)/shard_map/ppermute | solution.py:34
  91.9 2.8 %collective-permute-done.8 = f32[4,128]{1,0:T(4,128)S(1)} collective-permute-done((f32[4,128]{1,0:T(4,128)S(1)}, f32[4,128]{1,0:T(4,128)S(1)}, u32[]{:S(2)}, u32[]{:S(2)}) %collective-permute-start.8) | collective-permute-done | bytes 2080 | tf_op jit(solution)/shard_map/ppermute | solution.py:34
  95.1 28.3 %all-gather.1 = f32[16,4,128]{2,1,0:T(4,128)S(1)} all-gather(f32[1,4,128]{2,1,0:T(4,128)S(1)} %convolution_bitcast_fusion.2), channel_id=2, replica_groups=mesh['row'=16,'col'=32] {'row'}, dimensions={0}, use_global_device_ids=true | all-gather | bytes 34816 | tf_op jit(solution)/shard_map/all_gather | solution.py:119
  123.3 0.6 convolution_bitcast_fusion.1
  124.1 0.2 fusion.11
  124.3 0.2 convolution_add_fusion.8
  124.4 0.2 fusion.10
  124.6 0.2 convolution_add_fusion.6
  124.8 0.2 fusion.9
  125.0 0.2 convolution_add_fusion.4
  125.1 0.2 fusion.8
  125.3 0.2 convolution_add_fusion.2
  125.5 0.2 fusion.7
  125.7 0.4 fusion.24
  126.1 1.8 %fusion.5 = bf16[4,256,256]{1,2,0:T(8,128)(2,1)} fusion(f32[4,256,256]{1,2,0:T(8,128)S(1)} %fusion.12, f32[4,64,256]{2,1,0:T(8,128)S(1)} %fusion.24, f32[256,64]{0,1:T(8,128)S(1)} %copy-done.11), kind=kOutput, calls=%fused_computation.12 | convolution fusion | flops 201850880 | bytes 1900544 | tf_op jit(solution)/shard_map/ne,fel->fnl/dot_general | solution.py:138
  (53 shorter events, 1.9 us)
Async XLA Ops:
  0.0 123.3 %copy-start = (f32[2048,128]{1,0:T(8,128)S(1)}, f32[2048,128]{1,0:T(8,128)}, u32[]{:S(2)}) copy-start(f32[2048,128]{1,0:T(8,128)} %param.21) | copy-start | bytes 3145732
  3.1 7.9 %collective-permute-start = (bf16[4,16,16,1,64]{4,1,3,2,0:T(8,128)(2,1)S(1)}, bf16[4,16,16,1,64]{4,1,3,2,0:T(8,128)(2,1)S(1)}, u32[]{:S(2)}, u32[]{:S(2)}) collective-permute-start(bf16[4,16,16,1,64]{4,1,3,2,0:T(8,128)(2,1)S(1)} %copy.84), channel_id=1, source_target_pairs={{0,32},{32,64},{64,96},{96,128},{128,160},{160,192},{192,224},{224... | collective-permute-start | bytes 393224 | tf_op jit(solution)/shard_map/ppermute | solution.py:21
  6.7 5.8 %collective-permute-start.1 = (bf16[4,16,16,1,64]{4,1,3,2,0:T(8,128)(2,1)S(1)}, bf16[4,16,16,1,64]{4,1,3,2,0:T(8,128)(2,1)S(1)}, u32[]{:S(2)}, u32[]{:S(2)}) collective-permute-start(bf16[4,16,16,1,64]{4,1,3,2,0:T(8,128)(2,1)S(1)} %copy.85), channel_id=1, source_target_pairs={{32,0},{64,32},{96,64},{128,96},{160,128},{192,160},{224,192},{256... | collective-permute-start | bytes 393224 | tf_op jit(solution)/shard_map/ppermute | solution.py:22
  12.6 2.4 %copy-start.2 = (bf16[4,16,16,6,64]{4,1,3,2,0:T(8,128)(2,1)}, bf16[4,16,16,6,64]{4,1,3,2,0:T(8,128)(2,1)S(1)}, u32[]{:S(2)}) copy-start(bf16[4,16,16,6,64]{4,1,3,2,0:T(8,128)(2,1)S(1)} %constant_dynamic-update-slice_fusion) | copy-start | bytes 2359300
  14.9 17.1 %copy-start.4 = (f32[5,128,256]{2,1,0:T(8,128)S(1)}, f32[5,128,256]{2,1,0:T(8,128)}, u32[]{:S(2)}) copy-start(f32[5,128,256]{2,1,0:T(8,128)} %param.20) | copy-start | bytes 1966084
  18.6 13.6 %collective-permute-start.2 = (bf16[4,16,16,6,1]{2,1,4,3,0:T(8,128)(2,1)S(1)}, bf16[4,16,16,6,1]{2,1,4,3,0:T(8,128)(2,1)}, u32[]{:S(2)}, u32[]{:S(2)}) collective-permute-start(bf16[4,16,16,6,1]{2,1,4,3,0:T(8,128)(2,1)S(1)} %copy.58), channel_id=1, source_target_pairs={{0,1},{1,2},{2,3},{3,4},{4,5},{5,6},{6,7},{7,8},{8,9},{9,10},{10,1... | collective-permute-start | bytes 36872 | tf_op jit(solution)/shard_map/ppermute | solution.py:21
  26.0 10.8 %collective-permute-start.3 = (bf16[4,16,16,6,1]{2,1,4,3,0:T(8,128)(2,1)}, bf16[4,16,16,6,1]{2,1,4,3,0:T(8,128)(2,1)}, u32[]{:S(2)}, u32[]{:S(2)}) collective-permute-start(bf16[4,16,16,6,1]{2,1,4,3,0:T(8,128)(2,1)} %copy.59), channel_id=1, source_target_pairs={{1,0},{2,1},{3,2},{4,3},{5,4},{6,5},{7,6},{8,7},{9,8},{10,9},{11,1... | collective-permute-start | bytes 36872 | tf_op jit(solution)/shard_map/ppermute | solution.py:22
  45.2 0.7 copy-start.14
  51.8 1.6 %copy-start.1 = (f32[4,14,16,6,66]{4,1,3,2,0:T(8,128)}, f32[4,14,16,6,66]{4,1,3,2,0:T(8,128)S(1)}, u32[]{:S(2)}) copy-start(f32[4,14,16,6,66]{4,1,3,2,0:T(8,128)S(1)} %slice.198) | copy-start | bytes 4257796
  53.4 1.7 %copy-start.3 = (f32[4,16,16,6,66]{4,1,3,2,0:T(8,128)}, f32[4,16,16,6,66]{4,1,3,2,0:T(8,128)S(1)}, u32[]{:S(2)}) copy-start(f32[4,16,16,6,66]{4,1,3,2,0:T(8,128)S(1)} %pad_maximum_fusion) | copy-start | bytes 4866052
  56.1 2.1 %slice-start = ((f32[4,16,16,6,66]{4,1,3,2,0:T(8,128)}), f32[4,16,14,6,66]{4,1,3,2,0:T(8,128)S(1)}, s32[]{:S(2)}) async-start(f32[4,16,16,6,66]{4,1,3,2,0:T(8,128)} %copy-done.3), calls=%async_computation | async-start | bytes 5505024 | tf_op jit(solution)/shard_map/slice | solution.py:70
  62.1 2.6 %copy-start.10 = (f32[64,256]{1,0:T(8,128)S(1)}, f32[64,256]{1,0:T(8,128)}, u32[]{:S(2)}) copy-start(f32[64,256]{1,0:T(8,128)} %param.15) | copy-start | bytes 196612
  62.1 3.4 %copy-start.8 = (f32[256,128]{1,0:T(8,128)S(1)}, f32[256,128]{1,0:T(8,128)}, u32[]{:S(2)}) copy-start(f32[256,128]{1,0:T(8,128)} %param.17) | copy-start | bytes 393220
  62.1 3.4 %copy-start.12 = (f32[64,128]{1,0:T(8,128)S(1)}, f32[64,128]{1,0:T(8,128)}, u32[]{:S(2)}) copy-start(f32[64,128]{1,0:T(8,128)} %param.16) | copy-start | bytes 98308
  62.1 5.9 %copy-start.7 = (f32[256,256]{1,0:T(8,128)S(1)}, f32[256,256]{1,0:T(8,128)}, u32[]{:S(2)}) copy-start(f32[256,256]{1,0:T(8,128)} %param.14) | copy-start | bytes 786436
  64.7 5.7 %copy-start.5 = (f32[5,256,128]{2,1,0:T(8,128)S(1)}, f32[5,256,128]{2,1,0:T(8,128)}, u32[]{:S(2)}) copy-start(f32[5,256,128]{2,1,0:T(8,128)} %param.19) | copy-start | bytes 1966084
  64.7 7.8 %copy-start.6 = (f32[5,128,128]{2,1,0:T(8,128)S(1)}, f32[5,128,128]{2,1,0:T(8,128)}, u32[]{:S(2)}) copy-start(f32[5,128,128]{2,1,0:T(8,128)} %param.18) | copy-start | bytes 983044
  65.9 59.7 %copy-start.9 = (f32[256,128]{1,0:T(8,128)S(1)}, f32[256,128]{1,0:T(8,128)}, u32[]{:S(2)}) copy-start(f32[256,128]{1,0:T(8,128)} %param.23) | copy-start | bytes 393220
  65.9 59.8 %copy-start.13 = (f32[64,128]{1,0:T(8,128)S(1)}, f32[64,128]{1,0:T(8,128)}, u32[]{:S(2)}) copy-start(f32[64,128]{1,0:T(8,128)} %param.22) | copy-start | bytes 98308
  65.9 4.5 %collective-permute-start.4 = (f32[4,128]{1,0:T(4,128)S(1)}, f32[4,128]{1,0:T(4,128)S(1)}, u32[]{:S(2)}, u32[]{:S(2)}) collective-permute-start(f32[4,128]{1,0:T(4,128)S(1)} %fusion.6), channel_id=1, source_target_pairs={{0,1},{1,0},{2,3},{3,2},{4,5},{5,4},{6,7},{7,6},{8,9},{9,8},{10,11... | collective-permute-start | bytes 6152 | tf_op jit(solution)/shard_map/ppermute | solution.py:34
  69.1 57.0 %copy-start.11 = (f32[256,64]{0,1:T(8,128)S(1)}, f32[256,64]{0,1:T(8,128)}, u32[]{:S(2)}) copy-start(f32[256,64]{0,1:T(8,128)} %param.24) | copy-start | bytes 196612
  70.6 5.2 %collective-permute-start.5 = (f32[4,128]{1,0:T(4,128)S(1)}, f32[4,128]{1,0:T(4,128)S(1)}, u32[]{:S(2)}, u32[]{:S(2)}) collective-permute-start(f32[4,128]{1,0:T(4,128)S(1)} %fusion.33), channel_id=1, source_target_pairs={{0,2},{2,0},{1,3},{3,1},{4,6},{6,4},{5,7},{7,5},{8,10},{10,8},{9,1... | collective-permute-start | bytes 6152 | tf_op jit(solution)/shard_map/ppermute | solution.py:34
  76.0 8.2 %collective-permute-start.6 = (f32[4,128]{1,0:T(4,128)S(1)}, f32[4,128]{1,0:T(4,128)S(1)}, u32[]{:S(2)}, u32[]{:S(2)}) collective-permute-start(f32[4,128]{1,0:T(4,128)S(1)} %fusion.31), channel_id=1, source_target_pairs={{0,4},{4,0},{1,5},{5,1},{2,6},{6,2},{3,7},{7,3},{8,12},{12,8},{9,1... | collective-permute-start | bytes 6152 | tf_op jit(solution)/shard_map/ppermute | solution.py:34
  84.4 4.3 %collective-permute-start.7 = (f32[4,128]{1,0:T(4,128)S(1)}, f32[4,128]{1,0:T(4,128)S(1)}, u32[]{:S(2)}, u32[]{:S(2)}) collective-permute-start(f32[4,128]{1,0:T(4,128)S(1)} %fusion.29), channel_id=1, source_target_pairs={{0,8},{8,0},{1,9},{9,1},{2,10},{10,2},{3,11},{11,3},{4,12},{12,4},... | collective-permute-start | bytes 6152 | tf_op jit(solution)/shard_map/ppermute | solution.py:34
  88.9 5.8 %collective-permute-start.8 = (f32[4,128]{1,0:T(4,128)S(1)}, f32[4,128]{1,0:T(4,128)S(1)}, u32[]{:S(2)}, u32[]{:S(2)}) collective-permute-start(f32[4,128]{1,0:T(4,128)S(1)} %fusion.27), channel_id=1, source_target_pairs={{0,16},{16,0},{1,17},{17,1},{2,18},{18,2},{3,19},{19,3},{4,20},{20... | collective-permute-start | bytes 6152 | tf_op jit(solution)/shard_map/ppermute | solution.py:34
where the time goes:
time: 128 us
  local copies, waits for them, and re-layouts  33.6 us (26%)
  starting transfers between devices  29.6 us (23%)
  blocking collectives  28.3 us (22%)
  waiting for transfers between devices  13.9 us (11%)
  matrix products  13.4 us (10%)
  other arithmetic  8.61 us (7%)
    all_gather x1, blocking collectives, local(): shard_piece = lax.all_gather(skeleton[None], 'row', axis=0, tiled=True)  28.3 us
    ppermute x5, starting transfers between devices, partner_2(): return lax.ppermute(block, axis, route)  13.5 us
    ppermute x5, waiting for transfers between devices, partner_2(): return lax.ppermute(block, axis, route)  12.8 us
    ppermute x2, starting transfers between devices, extended(): after = lax.ppermute(first, axis, down)  9.4 us
    ppermute x2, starting transfers between devices, extended(): before = lax.ppermute(last, axis, up)  6.69 us
    slice x2, local copies, waits for them, and re-layouts, extended(): last = lax.slice_in_dim(x, length - width, length, axis=dim)  6.02 us
    slice x2, local copies, waits for them, and re-layouts, extended(): first = lax.slice_in_dim(x, 0, width, axis=dim)  4.95 us
    ppermute x1, local copies, waits for them, and re-layouts, extended(): before = lax.ppermute(last, axis, up)  4.6 us
  transfers between devices with their start and end apart: 9, of which 7 were waited for; matrix products, arithmetic and copies ran while one was open for 9% of the time, Pallas kernels for 0%

commit v1 on v0

--- a/solution.py
+++ b/solution.py
@@ -116,7 +116,9 @@
         )
         joined = jnp.concatenate([left_half, right_half], axis=-1)
         skeleton = jnp.dot(joined, merge_parent[merge_level], precision=full_precision)
-    shard_piece = lax.all_gather(skeleton[None], "row", axis=0, tiled=True)
+    shard_piece = jnp.concatenate(
+        lax.all_to_all(jnp.stack([skeleton[None]] * lax.axis_size("row")), "row", 0, 0), axis=0
+    )
     piece_rows = shard_piece.shape[0]
     top_rows = top_inverse
     top_rows = top_rows.reshape(piece_rows, SKEL, SKEL)

time: 128 us -> 127 us (level)
  blocking collectives: 28.3 us -> 0 us
  starting transfers between devices: 29.6 us -> 46.6 us
  matrix products: 13.4 us -> 18.5 us
  waiting for transfers between devices: 13.9 us -> 18.9 us
    all_gather x1 -> x0, blocking collectives: 28.3 us -> none  [local(): shard_piece = lax.all_gather(skeleton[None], 'row', axis=0, tiled=True)]
    all_to_all x0 -> x1, starting transfers between devices: none -> 16.7 us  [local(): lax.all_to_all(jnp.stack([skeleton[None]] * lax.axis_size('row')), 'row',...]
    all_to_all x0 -> x1, waiting for transfers between devices: none -> 6.4 us  [local(): lax.all_to_all(jnp.stack([skeleton[None]] * lax.axis_size('row')), 'row',...]
    dot_general x5, matrix products: 0.84 us -> 2.52 us  [local(): jnp.dot(boundary, child_map[:, :SKEL], precision=full_precision)]
    dot_general x5, matrix products: 0.87 us -> 2.54 us  [local(): jnp.dot(boundary, child_map[:, SKEL:], precision=full_precision)]
    ppermute x5, waiting for transfers between devices: 12.8 us -> 11.4 us  [partner_2(): return lax.ppermute(block, axis, route)]
    unnamed x34 -> x32, local copies, waits for them, and re-layouts: 3.93 us -> 3.94 us
  transfers between devices with their start and end apart: 9 -> 10, of which waited for: 7 -> 8; matrix products, arithmetic and copies ran while one was open for 9% -> 11% of each run, Pallas kernels for 0% -> 0%
where the time goes in v1:
time: 127 us; the launch traced here: 126 us
  starting transfers between devices  46.6 us (37%)
  local copies, waits for them, and re-layouts  32.8 us (26%)
  waiting for transfers between devices  18.9 us (15%)
  matrix products  18.5 us (15%)
  other arithmetic  8.61 us (7%)
    all_to_all x1, starting transfers between devices, local(): lax.all_to_all(jnp.stack([skeleton[None]] * lax.axis_size('row')), 'row',...  16.7 us
    ppermute x5, starting transfers between devices, partner_2(): return lax.ppermute(block, axis, route)  13.8 us
    ppermute x5, waiting for transfers between devices, partner_2(): return lax.ppermute(block, axis, route)  11.4 us
    ppermute x2, starting transfers between devices, extended(): after = lax.ppermute(first, axis, down)  9.4 us
    ppermute x2, starting transfers between devices, extended(): before = lax.ppermute(last, axis, up)  6.68 us
    all_to_all x1, waiting for transfers between devices, local(): lax.all_to_all(jnp.stack([skeleton[None]] * lax.axis_size('row')), 'row',...  6.4 us
    slice x2, local copies, waits for them, and re-layouts, extended(): last = lax.slice_in_dim(x, length - width, length, axis=dim)  6.04 us
    slice x2, local copies, waits for them, and re-layouts, extended(): first = lax.slice_in_dim(x, 0, width, axis=dim)  4.34 us
  transfers between devices with their start and end apart: 10, of which 8 were waited for; matrix products, arithmetic and copies ran while one was open for 11% of the time, Pallas kernels for 0%

profile of v1, /device:TPU:1, one launch (start us, length us, event | category | flops | bytes accessed | tf_op | source)
XLA Modules:
  0.0 125.8 jit_solution(4987139288974259671)
XLA Ops:
  0.0 2.1 %reshape.43 = bf16[4,16,16,4,64]{4,3,2,1,0:T(4,128)(2,1)S(1)} reshape(bf16[4,16,16,1,1,256]{5,2,4,3,1,0:T(8,128)(2,1)} %param.13) | data formatting | bytes 1048576 | tf_op jit(solution)/shard_map/reshape | solution.py:91
  2.1 0.7 fusion.102
  2.9 0.2 copy.84
  3.1 3.5 %collective-permute-start = (bf16[4,16,16,1,64]{4,1,3,2,0:T(8,128)(2,1)S(1)}, bf16[4,16,16,1,64]{4,1,3,2,0:T(8,128)(2,1)S(1)}, u32[]{:S(2)}, u32[]{:S(2)}) collective-permute-start(bf16[4,16,16,1,64]{4,1,3,2,0:T(8,128)(2,1)S(1)} %copy.84), channel_id=1, source_target_pairs={{0,32},{32,64},{64,96},{96,128},{128,160},{160,192},{192,224},{224... | collective-permute-start | bytes 393224 | tf_op jit(solution)/shard_map/ppermute | solution.py:21
  6.5 0.2 copy.85
  6.7 3.4 %collective-permute-start.1 = (bf16[4,16,16,1,64]{4,1,3,2,0:T(8,128)(2,1)S(1)}, bf16[4,16,16,1,64]{4,1,3,2,0:T(8,128)(2,1)S(1)}, u32[]{:S(2)}, u32[]{:S(2)}) collective-permute-start(bf16[4,16,16,1,64]{4,1,3,2,0:T(8,128)(2,1)S(1)} %copy.85), channel_id=1, source_target_pairs={{32,0},{64,32},{96,64},{128,96},{160,128},{192,160},{224,192},{256... | collective-permute-start | bytes 393224 | tf_op jit(solution)/shard_map/ppermute | solution.py:22
  10.1 0.8 collective-permute-done
  11.0 1.3 %constant_dynamic-update-slice_fusion.1 = bf16[4,16,16,6,64]{4,1,3,2,0:T(8,128)(2,1)S(1)} fusion(bf16[4,16,16,6,64]{4,1,3,2,0:T(8,128)(2,1)S(1)} %constant_dynamic-update-slice_fusion.2, bf16[4,16,16,4,64]{4,3,2,1,0:T(4,128)(2,1)S(1)} %reshape.43), kind=kLoop, calls=%fused_computation.111 | loop fusion | bytes 2097152
  12.2 0.3 collective-permute-done.1
  12.6 2.4 %fusion.101 = (bf16[4,16,16,6,1]{4,1,3,2,0:T(8,128)(2,1)}, bf16[4,16,16,6,1]{4,1,3,2,0:T(8,128)(2,1)}) fusion(bf16[4,16,16,6,64]{4,1,3,2,0:T(8,128)(2,1)S(1)} %constant_dynamic-update-slice_fusion), kind=kLoop, calls=%fused_computation.151 | loop fusion | bytes 49152 | tf_op jit(solution)/shard_map/slice | solution.py:19
  15.0 3.7 %copy.58 = bf16[4,16,16,6,1]{2,1,4,3,0:T(8,128)(2,1)S(1)} copy(bf16[4,16,16,6,1]{4,1,3,2,0:T(8,128)(2,1)} %get-tuple-element.19) | data formatting | bytes 24576 | tf_op jit(solution)/shard_map/slice | solution.py:19
  18.6 3.2 %collective-permute-start.2 = (bf16[4,16,16,6,1]{2,1,4,3,0:T(8,128)(2,1)S(1)}, bf16[4,16,16,6,1]{2,1,4,3,0:T(8,128)(2,1)S(1)}, u32[]{:S(2)}, u32[]{:S(2)}) collective-permute-start(bf16[4,16,16,6,1]{2,1,4,3,0:T(8,128)(2,1)S(1)} %copy.58), channel_id=1, source_target_pairs={{0,1},{1,2},{2,3},{3,4},{4,5},{5,6},{6,7},{7,8},{8,9},{9,10},{10,1... | collective-permute-start | bytes 36872 | tf_op jit(solution)/shard_map/ppermute | solution.py:21
  21.8 3.6 %copy.59 = bf16[4,16,16,6,1]{2,1,4,3,0:T(8,128)(2,1)S(1)} copy(bf16[4,16,16,6,1]{4,1,3,2,0:T(8,128)(2,1)} %get-tuple-element.20) | data formatting | bytes 24576 | tf_op jit(solution)/shard_map/slice | solution.py:20
  25.4 6.0 %collective-permute-start.3 = (bf16[4,16,16,6,1]{2,1,4,3,0:T(8,128)(2,1)S(1)}, bf16[4,16,16,6,1]{2,1,4,3,0:T(8,128)(2,1)S(1)}, u32[]{:S(2)}, u32[]{:S(2)}) collective-permute-start(bf16[4,16,16,6,1]{2,1,4,3,0:T(8,128)(2,1)S(1)} %copy.59), channel_id=1, source_target_pairs={{1,0},{2,1},{3,2},{4,3},{5,4},{6,5},{7,6},{8,7},{9,8},{10,9},{11,1... | collective-permute-start | bytes 36872 | tf_op jit(solution)/shard_map/ppermute | solution.py:22
  31.5 0.8 slice_bitcast_fusion.2
  32.2 3.8 %copy.60 = bf16[4,16,16,6,1]{4,1,3,2,0:T(8,128)(2,1)} copy(bf16[4,16,16,6,1]{2,1,4,3,0:T(8,128)(2,1)S(1)} %collective-permute-done.2) | data formatting | bytes 24576 | tf_op jit(solution)/shard_map/ppermute | solution.py:21
  36.0 3.8 %copy.61 = bf16[4,16,16,6,1]{4,1,3,2,0:T(8,128)(2,1)} copy(bf16[4,16,16,6,1]{2,1,4,3,0:T(8,128)(2,1)S(1)} %collective-permute-done.3) | data formatting | bytes 24576 | tf_op jit(solution)/shard_map/ppermute | solution.py:22
  39.9 3.8 %fusion.98 = (f32[4,16,16,6,66]{4,1,3,2,0:T(8,128)S(1)}, bf16[4,16,16,6,66]{4,1,3,2,0:T(8,128)(2,1)S(1)}) fusion(bf16[4,16,16,6,1]{4,1,3,2,0:T(8,128)(2,1)} %copy.61, bf16[4,16,16,6,64]{4,1,3,2,0:T(8,128)(2,1)} %copy-done.2, bf16[4,16,16,6,1]{4,1,3,2,0:T(8,128)(2,1)} %copy.60), kind=kLoop, calls=%fused_computation.148 | loop fusion | flops 2838528 | bytes 3244032 | tf_op jit(solution)/shard_map/convert_element_type | solution.py:93
  43.8 0.6 copy-done.13
  44.4 1.5 %fusion.3 = f32[4,16,6,66,16]{3,4,2,1,0:T(8,128)S(1)} fusion(f32[16,16,1,1,1]{1,0,4,3,2:T(8,128)S(1)} %copy-done.13, bf16[4,16,16,6,66]{4,1,3,2,0:T(8,128)(2,1)S(1)} %get-tuple-element.6), kind=kOutput, calls=%fused_computation.9 | convolution fusion | flops 77856768 | bytes 2434048 | tf_op jit(solution)/shard_map/jk,fikrc->fijrc/dot_general | solution.py:52
  45.9 3.5 %fusion.1 = f32[4,16,16,6,66]{4,1,3,2,0:T(8,128)S(1)} fusion(f32[4,16,6,66,16]{3,4,2,1,0:T(8,128)S(1)} %fusion.3, bf16[4,16,16,6,66]{4,1,3,2,0:T(8,128)(2,1)S(1)} %get-tuple-element.6, f32[16,16,1,1,1]{1,0,4,3,2:T(8,128)S(1)} %copy-done.13, f32[16,16,6,66]{3,0,2,1:T(8,128)S(1)} %get-tuple-element.18, f32[16,16,6,66]{3,0,2,1:T(8,128)S(1)} %get-tuple-element.17), kind=kOutput, calls=%fused_computation.3 | convolution fusion | flops 79478784 | bytes 4867072 | tf_op jit(solution)/shard_map/ik,fkjrc->fijrc/dot_general | solution.py:51
  49.3 0.3 fusion.99
  49.6 0.2 fusion.100
  49.8 0.4 slice.198
  50.3 0.7 fusion.22
  51.0 0.8 pad_maximum_fusion
  52.0 1.6 %copy-done.3 = f32[4,16,16,6,66]{4,1,3,2,0:T(8,128)} copy-done((f32[4,16,16,6,66]{4,1,3,2,0:T(8,128)}, f32[4,16,16,6,66]{4,1,3,2,0:T(8,128)S(1)}, u32[]{:S(2)}) %copy-start.3) | copy-done | bytes 1622040
  53.7 0.2 copy.70
  53.9 0.2 copy.71
  54.1 0.2 copy.68
  54.3 0.2 copy.69
  54.5 1.7 %fusion.19 = (f32[4,16,1,6,66]{4,1,3,2,0:T(8,128)S(1)}, f32[4,16,1,6,66]{4,1,3,2,0:T(8,128)S(1)}) fusion(f32[4,1,16,6,66]{4,1,3,2,0:T(1,128)S(1)} %get-tuple-element.12, f32[4,14,16,6,66]{4,1,3,2,0:T(8,128)} %copy-done.1, f32[4,1,16,6,66]{4,1,3,2,0:T(1,128)S(1)} %get-tuple-element.11, f32[4,16,1,6,1]{4,1,3,2,0:T(8,128)S(1)} %copy.69, ...), kind=kLoop, calls=%fused_computation.44 | loop fusion | flops 354816 | bytes 1827840 | tf_op jit(solution)/shard_map/mul | solution.py:67
  56.2 0.4 slice-done
  56.7 1.5 %fusion.2 = f32[4,16,16,4,64]{4,1,3,2,0:T(8,128)S(1)} fusion(f32[4,16,1,6,66]{4,1,3,2,0:T(8,128)S(1)} %get-tuple-element.8, f32[4,16,14,6,66]{4,1,3,2,0:T(8,128)S(1)} %slice-done, f32[4,16,1,6,66]{4,1,3,2,0:T(8,128)S(1)} %get-tuple-element.7, bf16[4,16,16,4,64]{4,3,2,1,0:T(4,128)(2,1)S(1)} %reshape.43), kind=kLoop, calls=%fused_computation.6 | loop fusion | flops 1048576 | bytes 3194880 | tf_op jit(solution)/shard_map/sub | solution.py:100
  58.2 2.4 %copy.72 = f32[4,16,16,4,64]{4,3,2,1,0:T(4,128)} copy(f32[4,16,16,4,64]{4,1,3,2,0:T(8,128)S(1)} %fusion.2) | data formatting | bytes 2097152 | tf_op jit(solution)/shard_map/sub | solution.py:100
  60.6 2.5 %reshape.44 = f32[4,256,256]{2,1,0:T(8,128)S(1)} reshape(f32[4,16,16,4,64]{4,3,2,1,0:T(4,128)} %copy.72) | data formatting | bytes 2097152 | tf_op jit(solution)/shard_map/reshape | solution.py:100
  63.1 0.8 convolution_bitcast_fusion
  63.9 0.4 fusion.6
  64.3 1.9 %collective-permute-start.4 = (f32[4,128]{1,0:T(4,128)S(1)}, f32[4,128]{1,0:T(4,128)S(1)}, u32[]{:S(2)}, u32[]{:S(2)}) collective-permute-start(f32[4,128]{1,0:T(4,128)S(1)} %fusion.6), channel_id=1, source_target_pairs={{0,1},{1,0},{2,3},{3,2},{4,5},{5,4},{6,7},{7,6},{8,9},{9,8},{10,11... | collective-permute-start | bytes 6152 | tf_op jit(solution)/shard_map/ppermute | solution.py:34
  66.2 2.0 %fusion.12 = f32[4,256,256]{1,2,0:T(8,128)S(1)} fusion(f32[4,256,256]{2,1,0:T(8,128)S(1)} %reshape.44, f32[256,256]{1,0:T(8,128)} %param.14), kind=kOutput, calls=%fused_computation.34 | convolution fusion | flops 805306368 | bytes 2359296 | tf_op jit(solution)/shard_map/nm,fml->fnl/dot_general | solution.py:101
  68.3 0.3 collective-permute-done.4
  68.8 2.4 %collective-permute-start.5 = (f32[4,128]{1,0:T(4,128)S(1)}, f32[4,128]{1,0:T(4,128)S(1)}, u32[]{:S(2)}, u32[]{:S(2)}) collective-permute-start(f32[4,128]{1,0:T(4,128)S(1)} %fusion.34), channel_id=1, source_target_pairs={{0,2},{2,0},{1,3},{3,1},{4,6},{6,4},{5,7},{7,5},{8,10},{10,8},{9,1... | collective-permute-start | bytes 6152 | tf_op jit(solution)/shard_map/ppermute | solution.py:34
  71.4 2.7 %collective-permute-done.5 = f32[4,128]{1,0:T(4,128)S(1)} collective-permute-done((f32[4,128]{1,0:T(4,128)S(1)}, f32[4,128]{1,0:T(4,128)S(1)}, u32[]{:S(2)}, u32[]{:S(2)}) %collective-permute-start.5) | collective-permute-done | bytes 2080 | tf_op jit(solution)/shard_map/ppermute | solution.py:34
  74.2 4.7 %collective-permute-start.6 = (f32[4,128]{1,0:T(4,128)S(1)}, f32[4,128]{1,0:T(4,128)S(1)}, u32[]{:S(2)}, u32[]{:S(2)}) collective-permute-start(f32[4,128]{1,0:T(4,128)S(1)} %fusion.32), channel_id=1, source_target_pairs={{0,4},{4,0},{1,5},{5,1},{2,6},{6,2},{3,7},{7,3},{8,12},{12,8},{9,1... | collective-permute-start | bytes 6152 | tf_op jit(solution)/shard_map/ppermute | solution.py:34
  79.1 3.3 %collective-permute-done.6 = f32[4,128]{1,0:T(4,128)S(1)} collective-permute-done((f32[4,128]{1,0:T(4,128)S(1)}, f32[4,128]{1,0:T(4,128)S(1)}, u32[]{:S(2)}, u32[]{:S(2)}) %collective-permute-start.6) | collective-permute-done | bytes 2080 | tf_op jit(solution)/shard_map/ppermute | solution.py:34
  82.6 1.9 %collective-permute-start.7 = (f32[4,128]{1,0:T(4,128)S(1)}, f32[4,128]{1,0:T(4,128)S(1)}, u32[]{:S(2)}, u32[]{:S(2)}) collective-permute-start(f32[4,128]{1,0:T(4,128)S(1)} %fusion.30), channel_id=1, source_target_pairs={{0,8},{8,0},{1,9},{9,1},{2,10},{10,2},{3,11},{11,3},{4,12},{12,4},... | collective-permute-start | bytes 6152 | tf_op jit(solution)/shard_map/ppermute | solution.py:34
  84.7 2.2 %collective-permute-done.7 = f32[4,128]{1,0:T(4,128)S(1)} collective-permute-done((f32[4,128]{1,0:T(4,128)S(1)}, f32[4,128]{1,0:T(4,128)S(1)}, u32[]{:S(2)}, u32[]{:S(2)}) %collective-permute-start.7) | collective-permute-done | bytes 2080 | tf_op jit(solution)/shard_map/ppermute | solution.py:34
  87.2 2.8 %collective-permute-start.8 = (f32[4,128]{1,0:T(4,128)S(1)}, f32[4,128]{1,0:T(4,128)S(1)}, u32[]{:S(2)}, u32[]{:S(2)}) collective-permute-start(f32[4,128]{1,0:T(4,128)S(1)} %fusion.28), channel_id=1, source_target_pairs={{0,16},{16,0},{1,17},{17,1},{2,18},{18,2},{3,19},{19,3},{4,20},{20... | collective-permute-start | bytes 6152 | tf_op jit(solution)/shard_map/ppermute | solution.py:34
  90.1 2.8 %collective-permute-done.8 = f32[4,128]{1,0:T(4,128)S(1)} collective-permute-done((f32[4,128]{1,0:T(4,128)S(1)}, f32[4,128]{1,0:T(4,128)S(1)}, u32[]{:S(2)}, u32[]{:S(2)}) %collective-permute-start.8) | collective-permute-done | bytes 2080 | tf_op jit(solution)/shard_map/ppermute | solution.py:34
  93.2 0.6 stack.3
  93.8 16.7 %all-to-all-start = ((f32[16,1,4,128]{3,2,1,0:T(4,128)}), f32[16,1,4,128]{3,2,1,0:T(4,128)S(1)}, u32[]{:S(2)}, u32[]{:S(2)}) async-start(f32[16,1,4,128]{3,2,1,0:T(4,128)} %stack.3), calls=%async_computation | async-start | bytes 65536 | tf_op jit(solution)/shard_map/all_to_all | solution.py:120
  110.5 1.0 fusion.62
  111.5 6.4 %all-to-all-done = f32[16,1,4,128]{3,2,1,0:T(4,128)S(1)} async-done(((f32[16,1,4,128]{3,2,1,0:T(4,128)}), f32[16,1,4,128]{3,2,1,0:T(4,128)S(1)}, u32[]{:S(2)}, u32[]{:S(2)}) %all-to-all-start) | async-done | bytes 32800 | tf_op jit(solution)/shard_map/all_to_all | solution.py:120
  117.9 0.6 convolution_bitcast_fusion.1
  118.5 1.0 convolution_add_fusion.10
  119.5 1.0 fusion.11
  120.5 1.0 convolution_add_fusion.8
  121.5 1.0 fusion.10
  122.7 0.2 fusion.9
  123.0 0.2 fusion.8
  123.2 0.2 convolution_add_fusion.2
  123.4 0.2 fusion.7
  123.6 0.4 fusion.24
  124.0 1.8 %fusion.5 = bf16[4,256,256]{1,2,0:T(8,128)(2,1)} fusion(f32[4,256,256]{1,2,0:T(8,128)S(1)} %fusion.12, f32[4,64,256]{2,1,0:T(8,128)S(1)} %fusion.24, f32[256,64]{0,1:T(8,128)S(1)} %copy-done.10), kind=kOutput, calls=%fused_computation.12 | convolution fusion | flops 201850880 | bytes 1900544 | tf_op jit(solution)/shard_map/ne,fel->fnl/dot_general | solution.py:140
  (53 shorter events, 2.4 us)
Async XLA Ops:
  0.0 117.9 %copy-start = (f32[2048,128]{1,0:T(8,128)S(1)}, f32[2048,128]{1,0:T(8,128)}, u32[]{:S(2)}) copy-start(f32[2048,128]{1,0:T(8,128)} %param.21) | copy-start | bytes 3145732
  3.1 7.9 %collective-permute-start = (bf16[4,16,16,1,64]{4,1,3,2,0:T(8,128)(2,1)S(1)}, bf16[4,16,16,1,64]{4,1,3,2,0:T(8,128)(2,1)S(1)}, u32[]{:S(2)}, u32[]{:S(2)}) collective-permute-start(bf16[4,16,16,1,64]{4,1,3,2,0:T(8,128)(2,1)S(1)} %copy.84), channel_id=1, source_target_pairs={{0,32},{32,64},{64,96},{96,128},{128,160},{160,192},{192,224},{224... | collective-permute-start | bytes 393224 | tf_op jit(solution)/shard_map/ppermute | solution.py:21
  6.7 5.8 %collective-permute-start.1 = (bf16[4,16,16,1,64]{4,1,3,2,0:T(8,128)(2,1)S(1)}, bf16[4,16,16,1,64]{4,1,3,2,0:T(8,128)(2,1)S(1)}, u32[]{:S(2)}, u32[]{:S(2)}) collective-permute-start(bf16[4,16,16,1,64]{4,1,3,2,0:T(8,128)(2,1)S(1)} %copy.85), channel_id=1, source_target_pairs={{32,0},{64,32},{96,64},{128,96},{160,128},{192,160},{224,192},{256... | collective-permute-start | bytes 393224 | tf_op jit(solution)/shard_map/ppermute | solution.py:22
  12.6 2.4 %copy-start.2 = (bf16[4,16,16,6,64]{4,1,3,2,0:T(8,128)(2,1)}, bf16[4,16,16,6,64]{4,1,3,2,0:T(8,128)(2,1)S(1)}, u32[]{:S(2)}) copy-start(bf16[4,16,16,6,64]{4,1,3,2,0:T(8,128)(2,1)S(1)} %constant_dynamic-update-slice_fusion) | copy-start | bytes 2359300
  15.0 16.5 %copy-start.4 = (f32[5,128,256]{2,1,0:T(8,128)S(1)}, f32[5,128,256]{2,1,0:T(8,128)}, u32[]{:S(2)}) copy-start(f32[5,128,256]{2,1,0:T(8,128)} %param.20) | copy-start | bytes 1966084
  18.6 13.6 %collective-permute-start.2 = (bf16[4,16,16,6,1]{2,1,4,3,0:T(8,128)(2,1)S(1)}, bf16[4,16,16,6,1]{2,1,4,3,0:T(8,128)(2,1)S(1)}, u32[]{:S(2)}, u32[]{:S(2)}) collective-permute-start(bf16[4,16,16,6,1]{2,1,4,3,0:T(8,128)(2,1)S(1)} %copy.58), channel_id=1, source_target_pairs={{0,1},{1,2},{2,3},{3,4},{4,5},{5,6},{6,7},{7,8},{8,9},{9,10},{10,1... | collective-permute-start | bytes 36872 | tf_op jit(solution)/shard_map/ppermute | solution.py:21
  25.4 10.6 %collective-permute-start.3 = (bf16[4,16,16,6,1]{2,1,4,3,0:T(8,128)(2,1)S(1)}, bf16[4,16,16,6,1]{2,1,4,3,0:T(8,128)(2,1)S(1)}, u32[]{:S(2)}, u32[]{:S(2)}) collective-permute-start(bf16[4,16,16,6,1]{2,1,4,3,0:T(8,128)(2,1)S(1)} %copy.59), channel_id=1, source_target_pairs={{1,0},{2,1},{3,2},{4,3},{5,4},{6,5},{7,6},{8,7},{9,8},{10,9},{11,1... | collective-permute-start | bytes 36872 | tf_op jit(solution)/shard_map/ppermute | solution.py:22
  43.7 0.7 copy-start.13
  50.2 1.6 %copy-start.1 = (f32[4,14,16,6,66]{4,1,3,2,0:T(8,128)}, f32[4,14,16,6,66]{4,1,3,2,0:T(8,128)S(1)}, u32[]{:S(2)}) copy-start(f32[4,14,16,6,66]{4,1,3,2,0:T(8,128)S(1)} %slice.198) | copy-start | bytes 4257796
  51.8 1.7 %copy-start.3 = (f32[4,16,16,6,66]{4,1,3,2,0:T(8,128)}, f32[4,16,16,6,66]{4,1,3,2,0:T(8,128)S(1)}, u32[]{:S(2)}) copy-start(f32[4,16,16,6,66]{4,1,3,2,0:T(8,128)S(1)} %pad_maximum_fusion) | copy-start | bytes 4866052
  54.5 2.1 %slice-start = ((f32[4,16,16,6,66]{4,1,3,2,0:T(8,128)}), f32[4,16,14,6,66]{4,1,3,2,0:T(8,128)S(1)}, s32[]{:S(2)}) async-start(f32[4,16,16,6,66]{4,1,3,2,0:T(8,128)} %copy-done.3), calls=%async_computation.1 | async-start | bytes 5505024 | tf_op jit(solution)/shard_map/slice | solution.py:70
  60.6 2.5 %copy-start.9 = (f32[64,256]{1,0:T(8,128)S(1)}, f32[64,256]{1,0:T(8,128)}, u32[]{:S(2)}) copy-start(f32[64,256]{1,0:T(8,128)} %param.15) | copy-start | bytes 196612
  60.6 3.4 %copy-start.7 = (f32[256,128]{1,0:T(8,128)S(1)}, f32[256,128]{1,0:T(8,128)}, u32[]{:S(2)}) copy-start(f32[256,128]{1,0:T(8,128)} %param.17) | copy-start | bytes 393220
  60.6 3.4 %copy-start.11 = (f32[64,128]{1,0:T(8,128)S(1)}, f32[64,128]{1,0:T(8,128)}, u32[]{:S(2)}) copy-start(f32[64,128]{1,0:T(8,128)} %param.16) | copy-start | bytes 98308
  63.1 5.6 %copy-start.5 = (f32[5,256,128]{2,1,0:T(8,128)S(1)}, f32[5,256,128]{2,1,0:T(8,128)}, u32[]{:S(2)}) copy-start(f32[5,256,128]{2,1,0:T(8,128)} %param.19) | copy-start | bytes 1966084
  63.1 8.1 %copy-start.6 = (f32[5,128,128]{2,1,0:T(8,128)S(1)}, f32[5,128,128]{2,1,0:T(8,128)}, u32[]{:S(2)}) copy-start(f32[5,128,128]{2,1,0:T(8,128)} %param.18) | copy-start | bytes 983044
  64.3 4.3 %collective-permute-start.4 = (f32[4,128]{1,0:T(4,128)S(1)}, f32[4,128]{1,0:T(4,128)S(1)}, u32[]{:S(2)}, u32[]{:S(2)}) collective-permute-start(f32[4,128]{1,0:T(4,128)S(1)} %fusion.6), channel_id=1, source_target_pairs={{0,1},{1,0},{2,3},{3,2},{4,5},{5,4},{6,7},{7,6},{8,9},{9,8},{10,11... | collective-permute-start | bytes 6152 | tf_op jit(solution)/shard_map/ppermute | solution.py:34
  68.3 55.3 %copy-start.8 = (f32[256,128]{1,0:T(8,128)S(1)}, f32[256,128]{1,0:T(8,128)}, u32[]{:S(2)}) copy-start(f32[256,128]{1,0:T(8,128)} %param.23) | copy-start | bytes 393220
  68.3 55.3 %copy-start.12 = (f32[64,128]{1,0:T(8,128)S(1)}, f32[64,128]{1,0:T(8,128)}, u32[]{:S(2)}) copy-start(f32[64,128]{1,0:T(8,128)} %param.22) | copy-start | bytes 98308
  68.3 55.7 %copy-start.10 = (f32[256,64]{0,1:T(8,128)S(1)}, f32[256,64]{0,1:T(8,128)}, u32[]{:S(2)}) copy-start(f32[256,64]{0,1:T(8,128)} %param.24) | copy-start | bytes 196612
  68.8 5.2 %collective-permute-start.5 = (f32[4,128]{1,0:T(4,128)S(1)}, f32[4,128]{1,0:T(4,128)S(1)}, u32[]{:S(2)}, u32[]{:S(2)}) collective-permute-start(f32[4,128]{1,0:T(4,128)S(1)} %fusion.34), channel_id=1, source_target_pairs={{0,2},{2,0},{1,3},{3,1},{4,6},{6,4},{5,7},{7,5},{8,10},{10,8},{9,1... | collective-permute-start | bytes 6152 | tf_op jit(solution)/shard_map/ppermute | solution.py:34
  74.2 8.2 %collective-permute-start.6 = (f32[4,128]{1,0:T(4,128)S(1)}, f32[4,128]{1,0:T(4,128)S(1)}, u32[]{:S(2)}, u32[]{:S(2)}) collective-permute-start(f32[4,128]{1,0:T(4,128)S(1)} %fusion.32), channel_id=1, source_target_pairs={{0,4},{4,0},{1,5},{5,1},{2,6},{6,2},{3,7},{7,3},{8,12},{12,8},{9,1... | collective-permute-start | bytes 6152 | tf_op jit(solution)/shard_map/ppermute | solution.py:34
  82.6 4.3 %collective-permute-start.7 = (f32[4,128]{1,0:T(4,128)S(1)}, f32[4,128]{1,0:T(4,128)S(1)}, u32[]{:S(2)}, u32[]{:S(2)}) collective-permute-start(f32[4,128]{1,0:T(4,128)S(1)} %fusion.30), channel_id=1, source_target_pairs={{0,8},{8,0},{1,9},{9,1},{2,10},{10,2},{3,11},{11,3},{4,12},{12,4},... | collective-permute-start | bytes 6152 | tf_op jit(solution)/shard_map/ppermute | solution.py:34
  87.2 5.8 %collective-permute-start.8 = (f32[4,128]{1,0:T(4,128)S(1)}, f32[4,128]{1,0:T(4,128)S(1)}, u32[]{:S(2)}, u32[]{:S(2)}) collective-permute-start(f32[4,128]{1,0:T(4,128)S(1)} %fusion.28), channel_id=1, source_target_pairs={{0,16},{16,0},{1,17},{17,1},{2,18},{18,2},{3,19},{19,3},{4,20},{20... | collective-permute-start | bytes 6152 | tf_op jit(solution)/shard_map/ppermute | solution.py:34
  93.8 24.1 %all-to-all-start = ((f32[16,1,4,128]{3,2,1,0:T(4,128)}), f32[16,1,4,128]{3,2,1,0:T(4,128)S(1)}, u32[]{:S(2)}, u32[]{:S(2)}) async-start(f32[16,1,4,128]{3,2,1,0:T(4,128)} %stack.3), calls=%async_computation | async-start | bytes 65536 | tf_op jit(solution)/shard_map/all_to_all | solution.py:120
